TPU v7x, 512 devices: a whole 4x8x8 slice. The times are simulated.
512 devices in a mesh: tm: 64 (over x, y, core), dp: 8 (over z).
Axes of the slice: x: 4, y: 8, z: 8, core: 2. Of those that a mesh axis runs over, the one named last changes fastest.
Arguments:
- frame_tokens: bfloat16 [8, 192, 64, 1280], P('dp', 'tm'), may hold values from -8 to 8
- visible: int32 [8, 192, 64], P('dp'), may hold values from 0 to 2
- grad_output: bfloat16 [8, 192, 64, 1280], P('dp', 'tm'), may hold values from -16 to 16
- norm_gain: float32 [1280], replicated, may hold values from 0.1 to 1.9
- query_weight: bfloat16 [1280, 640], P('tm'), may hold values from -1.5 to 1.5
- key_weight: bfloat16 [1280, 640], P('tm'), may hold values from -1.5 to 1.5
- value_weight: bfloat16 [1280, 640], P('tm'), may hold values from -0.15625 to 0.15625
- output_weight: bfloat16 [640, 1280], P('tm'), may hold values from -0.25 to 0.25
Outputs:
- block_out: bfloat16 [8, 192, 64, 1280], P('dp', 'tm')
- grad_tokens: bfloat16 [8, 192, 64, 1280], P('dp', 'tm')
- grad_output_weight: float32 [640, 1280], P('tm')
Inputs may be any that keep to these rules, and one draw needn't show every extreme that they name: visible[c, f, g] names which of the 3 cells of group g is visible in frame f.
All inputs are finite; a program needn't handle non-finite values.
Results may differ from a plain program's by a relative error of at most 0.012.
Values may be sent and summed in bfloat16 or wider, within the bound.
No kernel may reach another device: no remote copies, remote signals or barrier semaphores. Data moves between devices by JAX's collectives and lax.ppermute only.
A program may use at most 64 MiB of HBM per device.

v0:
```python
import math
import jax
import jax.numpy as jnp
from jax import lax
from jax.sharding import PartitionSpec as P

HEADS = 8
NORM_EPS = 1e-06


def normalize(token_rows, norm_gain):
    values = token_rows.astype(jnp.float32)
    centered = values - jnp.mean(values, axis=-1, keepdims=True)
    inverse = lax.rsqrt(jnp.mean(centered * centered, axis=-1, keepdims=True) + NORM_EPS)
    scaled = centered * inverse
    return (scaled, inverse, (scaled * norm_gain).astype(jnp.bfloat16))


def project(token_rows, weight):
    lead_shape = token_rows.shape[:-1]
    flat_rows = token_rows.reshape(-1, token_rows.shape[-1])
    result = jnp.dot(flat_rows, weight, preferred_element_type=jnp.float32)
    return result.astype(jnp.bfloat16).reshape(lead_shape + (weight.shape[1],))


def split_heads(values):
    return values.reshape(values.shape[:-1] + (HEADS, values.shape[-1] // HEADS))


def attend(query_rows, key_rows, value_rows, same_cell):
    score_scale = 1.0 / math.sqrt(query_rows.shape[-1] // HEADS)
    query_heads = split_heads(query_rows)
    key_heads = split_heads(key_rows)
    value_heads = split_heads(value_rows)
    scores = (
        jnp.einsum("fghe,tghe->ghft", query_heads, key_heads, preferred_element_type=jnp.float32)
        * score_scale
    )
    scores = jnp.where(same_cell[:, None], scores, -jnp.inf)
    row_top = jnp.max(scores, axis=-1, keepdims=True)
    expons = jnp.exp(scores - row_top)
    soft_probs = expons / jnp.sum(expons, axis=-1, keepdims=True)
    probs_low = soft_probs.astype(jnp.bfloat16)
    mixed_rows = jnp.einsum(
        "ghft,tghe->fghe", probs_low, value_heads, preferred_element_type=jnp.float32
    )
    return (soft_probs, probs_low, mixed_rows.reshape(query_rows.shape).astype(jnp.bfloat16))


def attend_back(query_rows, key_rows, value_rows, soft_probs, probs_low, grad_mixed):
    score_scale = 1.0 / math.sqrt(query_rows.shape[-1] // HEADS)
    query_heads = split_heads(query_rows)
    key_heads = split_heads(key_rows)
    value_heads = split_heads(value_rows)
    grad_heads = split_heads(grad_mixed)
    grad_probs = jnp.einsum(
        "fghe,tghe->ghft", grad_heads, value_heads, preferred_element_type=jnp.float32
    )
    centre = jnp.sum(soft_probs * grad_probs, axis=-1, keepdims=True)
    grad_scores = (soft_probs * (grad_probs - centre) * score_scale).astype(jnp.bfloat16)
    grad_query = jnp.einsum(
        "ghft,tghe->fghe", grad_scores, key_heads, preferred_element_type=jnp.float32
    )
    grad_key = jnp.einsum(
        "ghft,fghe->tghe", grad_scores, query_heads, preferred_element_type=jnp.float32
    )
    grad_value = jnp.einsum(
        "ghft,fghe->tghe", probs_low, grad_heads, preferred_element_type=jnp.float32
    )
    full_shape = query_rows.shape
    return (
        grad_query.reshape(full_shape).astype(jnp.bfloat16),
        grad_key.reshape(full_shape).astype(jnp.bfloat16),
        grad_value.reshape(full_shape).astype(jnp.bfloat16),
    )


def back_project(grad_query, grad_key, grad_value, query_weight, key_weight, value_weight):
    lead_shape = grad_query.shape[:-1]
    width = grad_query.shape[-1]
    total = jnp.dot(
        grad_query.reshape(-1, width), query_weight.T, preferred_element_type=jnp.float32
    )
    total = total + jnp.dot(
        grad_key.reshape(-1, width), key_weight.T, preferred_element_type=jnp.float32
    )
    total = total + jnp.dot(
        grad_value.reshape(-1, width), value_weight.T, preferred_element_type=jnp.float32
    )
    return total.astype(jnp.bfloat16).reshape(lead_shape + (query_weight.shape[0],))


def on_device(
    frame_tokens,
    visible,
    grad_output,
    norm_gain,
    query_weight,
    key_weight,
    value_weight,
    output_weight,
):
    query_weight, key_weight, value_weight, output_weight = (
        lax.all_gather(query_weight, "tm", axis=0, tiled=True),
        lax.all_gather(key_weight, "tm", axis=0, tiled=True),
        lax.all_gather(value_weight, "tm", axis=0, tiled=True),
        lax.all_gather(output_weight, "tm", axis=0, tiled=True),
    )
    shards = lax.axis_size("tm")
    tokens = frame_tokens[0]
    frame_count, visible_count, width = tokens.shape
    att_width = output_weight.shape[0]
    groups = visible_count // shards
    scaled, inverse, normed = normalize(tokens, norm_gain)
    local_cells = lax.dynamic_slice_in_dim(visible[0], lax.axis_index("tm") * groups, groups, 1)
    cell_major = local_cells.T
    same_cell = cell_major[:, :, None] == cell_major[:, None, :]
    query_rows = project(normed, query_weight)
    key_rows = project(normed, key_weight)
    value_rows = project(normed, value_weight)
    query_rows, key_rows, value_rows = (
        lax.all_to_all(query_rows, "tm", split_axis=1, concat_axis=0, tiled=True),
        lax.all_to_all(key_rows, "tm", split_axis=1, concat_axis=0, tiled=True),
        lax.all_to_all(value_rows, "tm", split_axis=1, concat_axis=0, tiled=True),
    )
    soft_probs, probs_low, mixed_cells = attend(query_rows, key_rows, value_rows, same_cell)
    mixed_frames = lax.all_to_all(mixed_cells, "tm", split_axis=0, concat_axis=1, tiled=True)
    flat_mixed = mixed_frames.reshape(-1, att_width)
    flat_tokens = tokens.reshape(-1, width)
    update = jnp.dot(flat_mixed, output_weight, preferred_element_type=jnp.float32)
    block_rows = (
        (flat_tokens.astype(jnp.float32) + update).astype(jnp.bfloat16).reshape(tokens.shape)
    )
    flat_grad = grad_output[0].reshape(-1, width)
    grad_mixed = jnp.dot(flat_grad, output_weight.T, preferred_element_type=jnp.float32)
    grad_mixed = grad_mixed.astype(jnp.bfloat16).reshape(frame_count, visible_count, att_width)
    term_share = lax.psum_scatter(
        jnp.dot(flat_mixed.T, flat_grad, preferred_element_type=jnp.float32),
        "tm",
        scatter_dimension=0,
        tiled=True,
    )
    grad_weight = lax.psum(term_share.astype(jnp.bfloat16), "dp").astype(jnp.float32)
    grad_cells = lax.all_to_all(grad_mixed, "tm", split_axis=1, concat_axis=0, tiled=True)
    grad_query, grad_key, grad_value = attend_back(
        query_rows, key_rows, value_rows, soft_probs, probs_low, grad_cells
    )
    grad_query, grad_key, grad_value = (
        lax.all_to_all(grad_query, "tm", split_axis=0, concat_axis=1, tiled=True),
        lax.all_to_all(grad_key, "tm", split_axis=0, concat_axis=1, tiled=True),
        lax.all_to_all(grad_value, "tm", split_axis=0, concat_axis=1, tiled=True),
    )
    grad_normed = back_project(
        grad_query, grad_key, grad_value, query_weight, key_weight, value_weight
    )
    weighted = grad_normed.astype(jnp.float32) * norm_gain
    first_mean = jnp.mean(weighted, axis=-1, keepdims=True)
    second_mean = jnp.mean(weighted * scaled, axis=-1, keepdims=True)
    grad_rows = inverse * (weighted - first_mean - scaled * second_mean) + grad_output[0].astype(
        jnp.float32
    )
    return (block_rows[None], grad_rows.astype(jnp.bfloat16)[None], grad_weight)


def solution(mesh):
    return jax.shard_map(
        on_device,
        mesh=mesh,
        in_specs=(
            P("dp", "tm", None, None),
            P("dp", None, None),
            P("dp", "tm", None, None),
            P(),
            P("tm", None),
            P("tm", None),
            P("tm", None),
            P("tm", None),
        ),
        out_specs=(P("dp", "tm", None, None), P("dp", "tm", None, None), P("tm", None)),
        check_vma=False,
    )
```

profile of v0, /device:TPU:64, one launch (start us, length us, event | category | flops | bytes accessed | tf_op | source)
XLA Modules:
  0.0 840.5 jit_solution(8921300924261810447)
XLA Ops:
  12.6 85.6 %all-gather.15.cloned.1.call-done = bf16[64,10,1280]{2,1,0:T(8,128)(2,1)} async-done(((bf16[1,10,1280]{2,1,0:T(8,128)(2,1)}), bf16[64,10,1280]{2,1,0:T(8,128)(2,1)}) %all-gather.15.cloned.1.call-update) | async-done | bytes 1638416 | tf_op jit(solution)/shard_map/all_gather | solution.py:107
  98.2 2.7 reshape.316
  102.6 6.7 all-to-all-start.4
  110.7 71.2 %all-gather.13.cloned.1.call-done = bf16[64,20,640]{2,1,0:T(8,128)(2,1)} async-done(((bf16[1,20,640]{2,1,0:T(8,128)(2,1)}), bf16[64,20,640]{2,1,0:T(8,128)(2,1)}) %all-gather.13.cloned.1.call-update) | async-done | bytes 1638416 | tf_op jit(solution)/shard_map/all_gather | solution.py:105
  181.9 2.4 reshape.314
  185.9 7.0 all-to-all-start.2
  192.9 72.7 %all-gather.11.cloned.1.call-done = bf16[64,20,640]{2,1,0:T(8,128)(2,1)} async-done(((bf16[1,20,640]{2,1,0:T(8,128)(2,1)}), bf16[64,20,640]{2,1,0:T(8,128)(2,1)}) %all-gather.11.cloned.1.call-update) | async-done | bytes 1638416 | tf_op jit(solution)/shard_map/all_gather | solution.py:104
  265.7 2.4 reshape.312
  270.7 7.0 all-to-all-start.1
  277.8 71.5 %all-gather.9.cloned.1.call-done = bf16[64,20,640]{2,1,0:T(8,128)(2,1)} async-done(((bf16[1,20,640]{2,1,0:T(8,128)(2,1)}), bf16[64,20,640]{2,1,0:T(8,128)(2,1)}) %all-gather.9.cloned.1.call-update) | async-done | bytes 1638416 | tf_op jit(solution)/shard_map/all_gather | solution.py:106
  349.3 3.6 reshape.310
  352.9 2.2 convolution_convert_fusion.5
  356.0 2.2 reshape.303
  358.2 2.0 copy.53
  360.2 2.2 reshape.300
  362.4 2.0 copy.47
  364.3 7.0 all-to-all-start
  371.3 2.2 reshape.298
  373.5 2.0 copy.46
  375.5 2.9 fusion.42
  378.4 2.6 convolution_convert_fusion
  381.6 2.5 reduce.16
  387.9 10.7 %all-to-all-start.7 = ((bf16[64,2,960]{2,1,0:T(2,128)(2,1)}), bf16[64,2,960]{2,1,0:T(2,128)(2,1)}, u32[]{:S(2)}, u32[]{:S(2)}) async-start(bf16[64,2,960]{2,1,0:T(2,128)(2,1)} %reshape.328), calls=%async_computation.7 | async-start | bytes 524288 | tf_op jit(solution)/shard_map/all_to_all | solution.py:151
  398.6 2.2 reshape.296
  400.8 2.0 copy.48
  402.8 2.5 convolution_convert_fusion.1
  405.3 2.5 reduce.13
  411.6 10.5 %all-to-all-start.3 = ((bf16[64,2,960]{2,1,0:T(2,128)(2,1)}), bf16[64,2,960]{2,1,0:T(2,128)(2,1)}, u32[]{:S(2)}, u32[]{:S(2)}) async-start(bf16[64,2,960]{2,1,0:T(2,128)(2,1)} %reshape.322), calls=%async_computation.3 | async-start | bytes 524288 | tf_op jit(solution)/shard_map/all_to_all | solution.py:127
  422.1 2.6 fusion.43
  424.7 4.3 fusion.19
  429.1 2.5 reduce.15
  435.3 10.5 %all-to-all-start.6 = ((bf16[64,2,960]{2,1,0:T(2,128)(2,1)}), bf16[64,2,960]{2,1,0:T(2,128)(2,1)}, u32[]{:S(2)}, u32[]{:S(2)}) async-start(bf16[64,2,960]{2,1,0:T(2,128)(2,1)} %reshape.326), calls=%async_computation.6 | async-start | bytes 524288 | tf_op jit(solution)/shard_map/all_to_all | solution.py:150
  447.8 4.4 fusion.16
  452.1 2.5 reduce.14
  456.5 2.0 reshape.324
  458.4 2.8 reshape.329
  461.3 3.1 reduce.12
  467.8 2.8 reshape.323
  470.7 3.1 reduce.9
  477.2 10.5 %all-to-all-start.5 = ((bf16[64,2,960]{2,1,0:T(2,128)(2,1)}), bf16[64,2,960]{2,1,0:T(2,128)(2,1)}, u32[]{:S(2)}, u32[]{:S(2)}) async-start(bf16[64,2,960]{2,1,0:T(2,128)(2,1)} %reshape.324), calls=%async_computation.5 | async-start | bytes 524288 | tf_op jit(solution)/shard_map/all_to_all | solution.py:149
  487.7 2.9 reshape.327
  490.6 3.1 reduce.11
  497.1 3.0 fusion.2
  500.1 2.3 fusion.45
  502.5 2.8 reshape.325
  505.3 3.1 reduce.10
  514.9 287.3 %all-reduce.2 = bf16[640,1280]{1,0:T(8,128)(2,1)} all-reduce(f32[640,1280]{1,0:T(8,128)} %fusion.45), channel_id=2, replica_groups=mesh['tm'=64,'dp'=8] {'tm'}, use_global_device_ids=true, to_apply=%region_7.8.clone | all-reduce | flops 819200 | bytes 4915200
  803.0 29.0 %psum.7 = bf16[10,1280]{1,0:T(8,128)(2,1)S(1)} all-reduce(bf16[10,1280]{1,0:T(8,128)(2,1)S(1)} %dynamic-slice_convert_fusion), channel_id=1, replica_groups=mesh['tm'=64,'dp'=8] {'dp'}, use_global_device_ids=true, to_apply=%region_8.9 | all-reduce | flops 12800 | bytes 51200 | tf_op jit(solution)/shard_map/psum | solution.py:143
  (88 shorter events, 48.0 us)
Async XLA Ops:
  7.2 185.7 %copy-start = (s32[1,192,64]{1,2,0:T(8,128)S(1)}, s32[1,192,64]{1,2,0:T(8,128)}, u32[]{:S(2)}) copy-start(s32[1,192,64]{1,2,0:T(8,128)} %param.9) | copy-start | bytes 147460
  7.2 91.1 %all-gather.15.cloned.1.call-start = ((), (), s32[]{:S(2)}) async-start(), calls=%async_computation.11 | async-start | bytes 2662400 | tf_op jit(solution)/shard_map/all_gather | solution.py:107
  7.9 174.0 %all-gather.13.cloned.1.call-start = ((), (), s32[]{:S(2)}) async-start(), calls=%async_computation.10 | async-start | bytes 1996800 | tf_op jit(solution)/shard_map/all_gather | solution.py:105
  8.7 257.0 %all-gather.11.cloned.1.call-start = ((), (), s32[]{:S(2)}) async-start(), calls=%async_computation.9 | async-start | bytes 1996800 | tf_op jit(solution)/shard_map/all_gather | solution.py:104
  9.4 339.9 %all-gather.9.cloned.1.call-start = ((), (), s32[]{:S(2)}) async-start(), calls=%async_computation.8 | async-start | bytes 1996800 | tf_op jit(solution)/shard_map/all_gather | solution.py:106
  12.6 88.3 %copy-start.6 = (bf16[1,3,64,1280]{3,2,1,0:T(8,128)(2,1)S(1)}, bf16[1,3,64,1280]{3,2,1,0:T(8,128)(2,1)}, u32[]{:S(2)}) copy-start(bf16[1,3,64,1280]{3,2,1,0:T(8,128)(2,1)} %param.10) | copy-start | bytes 1474564
  101.0 1.7 copy-start.2
  101.0 8.4 copy-start.3
  101.0 8.4 copy-start.14
  102.6 83.2 %all-to-all-start.4 = ((bf16[3,64,640]{2,0,1:T(4,128)(2,1)}), bf16[3,64,640]{2,0,1:T(4,128)(2,1)S(1)}, u32[]{:S(2)}, u32[]{:S(2)}) async-start(bf16[3,64,640]{2,0,1:T(4,128)(2,1)} %copy.52), calls=%async_computation.4 | async-start | bytes 655360 | tf_op jit(solution)/shard_map/all_to_all | solution.py:144
  110.7 73.6 %copy-start.5 = (bf16[192,1280]{1,0:T(8,128)(2,1)}, bf16[192,1280]{1,0:T(8,128)(2,1)S(1)}, u32[]{:S(2)}) copy-start(bf16[192,1280]{1,0:T(8,128)(2,1)S(1)} %get-tuple-element.6) | copy-start | bytes 1474564
  185.9 7.1 copy-start.11
  185.9 84.8 %all-to-all-start.2 = ((bf16[3,64,640]{2,0,1:T(4,128)(2,1)}), bf16[3,64,640]{2,0,1:T(4,128)(2,1)}, u32[]{:S(2)}, u32[]{:S(2)}) async-start(bf16[3,64,640]{2,0,1:T(4,128)(2,1)} %copy.45), calls=%async_computation.2 | async-start | bytes 655360 | tf_op jit(solution)/shard_map/all_to_all | solution.py:123
  270.7 93.7 %all-to-all-start.1 = ((bf16[3,64,640]{2,0,1:T(4,128)(2,1)}), bf16[3,64,640]{2,0,1:T(4,128)(2,1)}, u32[]{:S(2)}, u32[]{:S(2)}) async-start(bf16[3,64,640]{2,0,1:T(4,128)(2,1)} %copy.44), calls=%async_computation.1 | async-start | bytes 655360 | tf_op jit(solution)/shard_map/all_to_all | solution.py:122
  364.3 23.6 %all-to-all-start = ((bf16[3,64,640]{2,0,1:T(4,128)(2,1)}), bf16[3,64,640]{2,0,1:T(4,128)(2,1)}, u32[]{:S(2)}, u32[]{:S(2)}) async-start(bf16[3,64,640]{2,0,1:T(4,128)(2,1)} %copy.43), calls=%async_computation | async-start | bytes 655360 | tf_op jit(solution)/shard_map/all_to_all | solution.py:124
  387.9 23.7 %all-to-all-start.7 = ((bf16[64,2,960]{2,1,0:T(2,128)(2,1)}), bf16[64,2,960]{2,1,0:T(2,128)(2,1)}, u32[]{:S(2)}, u32[]{:S(2)}) async-start(bf16[64,2,960]{2,1,0:T(2,128)(2,1)} %reshape.328), calls=%async_computation.7 | async-start | bytes 524288 | tf_op jit(solution)/shard_map/all_to_all | solution.py:151
  411.6 23.8 %all-to-all-start.3 = ((bf16[64,2,960]{2,1,0:T(2,128)(2,1)}), bf16[64,2,960]{2,1,0:T(2,128)(2,1)}, u32[]{:S(2)}, u32[]{:S(2)}) async-start(bf16[64,2,960]{2,1,0:T(2,128)(2,1)} %reshape.322), calls=%async_computation.3 | async-start | bytes 524288 | tf_op jit(solution)/shard_map/all_to_all | solution.py:127
  435.3 41.9 %all-to-all-start.6 = ((bf16[64,2,960]{2,1,0:T(2,128)(2,1)}), bf16[64,2,960]{2,1,0:T(2,128)(2,1)}, u32[]{:S(2)}, u32[]{:S(2)}) async-start(bf16[64,2,960]{2,1,0:T(2,128)(2,1)} %reshape.326), calls=%async_computation.6 | async-start | bytes 524288 | tf_op jit(solution)/shard_map/all_to_all | solution.py:150
  477.2 25.3 %all-to-all-start.5 = ((bf16[64,2,960]{2,1,0:T(2,128)(2,1)}), bf16[64,2,960]{2,1,0:T(2,128)(2,1)}, u32[]{:S(2)}, u32[]{:S(2)}) async-start(bf16[64,2,960]{2,1,0:T(2,128)(2,1)} %reshape.324), calls=%async_computation.5 | async-start | bytes 524288 | tf_op jit(solution)/shard_map/all_to_all | solution.py:149
  497.1 3.0 copy-start.7
  497.1 3.0 copy-start.10
  511.2 0.9 copy-start.13
  512.1 1.4 copy-start.1
  512.1 1.7 copy-start.9
  512.1 1.7 copy-start.12
  514.9 317.8 %copy-start.4 = (bf16[1,3,64,1280]{3,2,1,0:T(8,128)(2,1)S(1)}, bf16[1,3,64,1280]{3,2,1,0:T(8,128)(2,1)}, u32[]{:S(2)}) copy-start(bf16[1,3,64,1280]{3,2,1,0:T(8,128)(2,1)} %param.8) | copy-start | bytes 1474564
  514.9 317.8 %copy-start.8 = (bf16[1,3,64,1280]{3,2,1,0:T(8,128)(2,1)S(1)}, bf16[1,3,64,1280]{3,2,1,0:T(8,128)(2,1)}, u32[]{:S(2)}) copy-start(bf16[1,3,64,1280]{3,2,1,0:T(8,128)(2,1)} %param.10) | copy-start | bytes 1474564
Sparse Core Ops, SparseCore 0:
  11.3 86.8 all-gather.14
  101.5 80.3 all-gather.12
  185.2 80.4 all-gather.10
  268.8 80.4 all-gather.8
where the time goes:
time: 843 us; the launch traced here: 840 us
  blocking collectives  316 us (37%)
  waiting for transfers between devices  304 us (36%)
  local copies, waits for them, and re-layouts  75.6 us (9%)
  starting transfers between devices  70.1 us (8%)
  matrix products  31.9 us (4%)
  other arithmetic  28.2 us (3%)
  between operations  14.7 us (2%)
    unnamed x1, blocking collectives  287 us
    all_gather x1, waiting for transfers between devices, on_device(): lax.all_gather(output_weight, 'tm', axis=0, tiled=True)  85.6 us
    all_gather x1, waiting for transfers between devices, on_device(): lax.all_gather(query_weight, 'tm', axis=0, tiled=True)  72.7 us
    all_gather x1, waiting for transfers between devices, on_device(): lax.all_gather(value_weight, 'tm', axis=0, tiled=True)  71.5 us
    all_gather x1, waiting for transfers between devices, on_device(): lax.all_gather(key_weight, 'tm', axis=0, tiled=True)  71.2 us
    unnamed x47, local copies, waits for them, and re-layouts  40.3 us
    psum x1, blocking collectives, on_device(): lax.psum(term_share.astype(jnp.bfloat16), 'dp').astype(jnp.float32)  29 us
  transfers between devices with their start and end apart: 12, of which 4 were waited for; matrix products, arithmetic and copies ran while one was open for 14% of the time, Pallas kernels for 0%

commit v1 on v0

--- a/solution.py
+++ b/solution.py
@@ -102,7 +102,9 @@
 ):
     query_weight, key_weight, value_weight, output_weight = (
         lax.all_gather(query_weight, "tm", axis=0, tiled=True),
-        lax.all_gather(key_weight, "tm", axis=0, tiled=True),
+        jnp.concatenate(
+            lax.all_to_all(jnp.stack([key_weight] * lax.axis_size("tm")), "tm", 0, 0), axis=0
+        ),
         lax.all_gather(value_weight, "tm", axis=0, tiled=True),
         lax.all_gather(output_weight, "tm", axis=0, tiled=True),
     )

time: 843 us -> 749 us (0.89)
  waiting for transfers between devices: 304 us -> 213 us
  local copies, waits for them, and re-layouts: 75.6 us -> 65.6 us
    all_gather x1 -> x0, waiting for transfers between devices: 71.2 us -> none  [on_device(): lax.all_gather(key_weight, 'tm', axis=0, tiled=True)]
    all_gather x1, waiting for transfers between devices: 71.5 us -> 53.4 us  [on_device(): lax.all_gather(value_weight, 'tm', axis=0, tiled=True)]
    all_gather x1, waiting for transfers between devices: 85.6 us -> 71 us  [on_device(): lax.all_gather(output_weight, 'tm', axis=0, tiled=True)]
    all_to_all x0 -> x1, starting transfers between devices: none -> 10.9 us  [on_device(): lax.all_to_all(jnp.stack([key_weight] * lax.axis_size('tm')), 'tm', 0, 0)]
    unnamed x47 -> x32, local copies, waits for them, and re-layouts: 40.3 us -> 36.3 us
    another operation x8 -> x9, local copies, waits for them, and re-layouts: 16.7 us -> 17.3 us
  transfers between devices with their start and end apart: 12 -> 12, of which waited for: 4 -> 8; matrix products, arithmetic and copies ran while one was open for 14% -> 12% of each run, Pallas kernels for 0% -> 0%
where the time goes in v1:
time: 749 us; the launch traced here: 746 us
  blocking collectives  316 us (42%)
  waiting for transfers between devices  213 us (28%)
  starting transfers between devices  77.3 us (10%)
  local copies, waits for them, and re-layouts  65.6 us (9%)
  matrix products  36.1 us (5%)
  other arithmetic  24.3 us (3%)
  between operations  14.7 us (2%)
    unnamed x1, blocking collectives  287 us
    all_gather x1, waiting for transfers between devices, on_device(): lax.all_gather(query_weight, 'tm', axis=0, tiled=True)  75 us
    all_gather x1, waiting for transfers between devices, on_device(): lax.all_gather(output_weight, 'tm', axis=0, tiled=True)  71 us
    all_gather x1, waiting for transfers between devices, on_device(): lax.all_gather(value_weight, 'tm', axis=0, tiled=True)  53.4 us
    unnamed x32, local copies, waits for them, and re-layouts  36.3 us
    psum x1, blocking collectives, on_device(): lax.psum(term_share.astype(jnp.bfloat16), 'dp').astype(jnp.float32)  29 us
    another operation x8, local copies, waits for them, and re-layouts  15 us
  transfers between devices with their start and end apart: 12, of which 8 were waited for; matrix products, arithmetic and copies ran while one was open for 12% of the time, Pallas kernels for 0%

profile of v1, /device:TPU:64, one launch (start us, length us, event | category | flops | bytes accessed | tf_op | source)
XLA Modules:
  0.0 746.2 jit_solution(12265748117038643734)
XLA Ops:
  8.7 2.2 stack.2
  10.9 10.9 %all-to-all-start.2 = ((bf16[64,20,640]{2,1,0:T(8,128)(2,1)}), bf16[64,20,640]{2,1,0:T(8,128)(2,1)}, u32[]{:S(2)}, u32[]{:S(2)}) async-start(bf16[64,20,640]{2,1,0:T(8,128)(2,1)} %stack.2), calls=%async_computation.2 | async-start | bytes 3932160 | tf_op jit(solution)/shard_map/all_to_all | solution.py:106
  23.5 75.0 %all-gather.9.cloned.1.call-done = bf16[64,20,640]{2,1,0:T(8,128)(2,1)} async-done(((bf16[1,20,640]{2,1,0:T(8,128)(2,1)}), bf16[64,20,640]{2,1,0:T(8,128)(2,1)}) %all-gather.9.cloned.1.call-update) | async-done | bytes 1638416 | tf_op jit(solution)/shard_map/all_gather | solution.py:104
  98.5 2.4 reshape.337
  102.5 6.8 all-to-all-start.1
  110.3 2.4 reshape.323
  115.3 7.1 all-to-all-done.1
  122.5 6.6 all-to-all-start.3
  129.0 53.4 %all-gather.7.cloned.1.call-done = bf16[64,20,640]{2,1,0:T(8,128)(2,1)} async-done(((bf16[1,20,640]{2,1,0:T(8,128)(2,1)}), bf16[64,20,640]{2,1,0:T(8,128)(2,1)}) %all-gather.7.cloned.1.call-update) | async-done | bytes 1638416 | tf_op jit(solution)/shard_map/all_gather | solution.py:108
  182.5 3.6 reshape.335
  186.1 2.0 convolution_convert_fusion.5
  189.0 7.0 all-to-all-start
  196.0 71.0 %all-gather.11.cloned.1.call-done = bf16[64,10,1280]{2,1,0:T(8,128)(2,1)} async-done(((bf16[1,10,1280]{2,1,0:T(8,128)(2,1)}), bf16[64,10,1280]{2,1,0:T(8,128)(2,1)}) %all-gather.11.cloned.1.call-update) | async-done | bytes 1638416 | tf_op jit(solution)/shard_map/all_gather | solution.py:109
  267.0 4.0 reshape.339
  271.0 2.3 convolution_convert_fusion.2
  274.2 7.1 all-to-all-start.5
  285.3 2.2 reshape.325
  287.5 2.0 copy.47
  289.5 2.2 reshape.320
  294.2 2.2 reshape.328
  296.4 2.0 copy.53
  298.4 2.5 fusion.45
  301.0 2.9 fusion.44
  303.9 4.3 fusion.19
  308.8 2.5 reduce.15
  313.1 2.0 reshape.349
  315.1 9.1 %all-to-all-start.7 = ((bf16[64,2,960]{2,1,0:T(2,128)(2,1)}), bf16[64,2,960]{2,1,0:T(2,128)(2,1)}, u32[]{:S(2)}, u32[]{:S(2)}) async-start(bf16[64,2,960]{2,1,0:T(2,128)(2,1)} %reshape.349), calls=%async_computation.7 | async-start | bytes 524288 | tf_op jit(solution)/shard_map/all_to_all | solution.py:152
  324.1 4.3 fusion.16
  328.5 2.5 reduce.14
  336.0 9.3 %all-to-all-start.6 = ((bf16[64,2,960]{2,1,0:T(2,128)(2,1)}), bf16[64,2,960]{2,1,0:T(2,128)(2,1)}, u32[]{:S(2)}, u32[]{:S(2)}) async-start(bf16[64,2,960]{2,1,0:T(2,128)(2,1)} %reshape.347), calls=%async_computation.6 | async-start | bytes 524288 | tf_op jit(solution)/shard_map/all_to_all | solution.py:151
  347.2 2.6 convolution_convert_fusion
  349.8 2.5 reduce.16
  354.2 2.0 reshape.351
  357.1 9.8 %all-to-all-start.8 = ((bf16[64,2,960]{2,1,0:T(2,128)(2,1)}), bf16[64,2,960]{2,1,0:T(2,128)(2,1)}, u32[]{:S(2)}, u32[]{:S(2)}) async-start(bf16[64,2,960]{2,1,0:T(2,128)(2,1)} %reshape.351), calls=%async_computation.8 | async-start | bytes 524288 | tf_op jit(solution)/shard_map/all_to_all | solution.py:153
  366.9 2.4 convolution_convert_fusion.1
  373.8 2.8 reshape.350
  376.7 3.1 reduce.11
  381.6 2.8 reshape.348
  384.4 3.1 reduce.10
  388.6 3.0 fusion.46
  391.6 10.6 %all-to-all-start.4 = ((bf16[64,2,960]{2,1,0:T(2,128)(2,1)}), bf16[64,2,960]{2,1,0:T(2,128)(2,1)}, u32[]{:S(2)}, u32[]{:S(2)}) async-start(bf16[64,2,960]{2,1,0:T(2,128)(2,1)} %reshape.345), calls=%async_computation.4 | async-start | bytes 524288 | tf_op jit(solution)/shard_map/all_to_all | solution.py:129
  402.2 2.9 reshape.352
  405.1 3.1 reduce.12
  409.3 2.1 convolution_add_fusion.1
  413.8 2.2 reshape.346
  417.6 2.3 fusion.47
  420.0 286.5 %all-reduce.2 = bf16[640,1280]{1,0:T(8,128)(2,1)} all-reduce(f32[640,1280]{1,0:T(8,128)} %fusion.47), channel_id=2, replica_groups=mesh['tm'=64,'dp'=8] {'tm'}, use_global_device_ids=true, to_apply=%region_7.8.clone | all-reduce | flops 819200 | bytes 4915200
  707.4 29.0 %psum.7 = bf16[10,1280]{1,0:T(8,128)(2,1)S(1)} all-reduce(bf16[10,1280]{1,0:T(8,128)(2,1)S(1)} %dynamic-slice_convert_fusion), channel_id=1, replica_groups=mesh['tm'=64,'dp'=8] {'dp'}, use_global_device_ids=true, to_apply=%region_8.9 | all-reduce | flops 12800 | bytes 51200 | tf_op jit(solution)/shard_map/psum | solution.py:145
  (75 shorter events, 44.4 us)
Async XLA Ops:
  7.2 274.2 %copy-start = (s32[1,192,64]{1,2,0:T(8,128)S(1)}, s32[1,192,64]{1,2,0:T(8,128)}, u32[]{:S(2)}) copy-start(s32[1,192,64]{1,2,0:T(8,128)} %param.9) | copy-start | bytes 147460
  7.2 91.3 %all-gather.9.cloned.1.call-start = ((), (), s32[]{:S(2)}) async-start(), calls=%async_computation.10 | async-start | bytes 1996800 | tf_op jit(solution)/shard_map/all_gather | solution.py:104
  7.9 174.5 %all-gather.7.cloned.1.call-start = ((), (), s32[]{:S(2)}) async-start(), calls=%async_computation.9 | async-start | bytes 1996800 | tf_op jit(solution)/shard_map/all_gather | solution.py:108
  10.9 11.7 %copy-start.1 = (bf16[1,3,64,1280]{3,2,1,0:T(8,128)(2,1)S(1)}, bf16[1,3,64,1280]{3,2,1,0:T(8,128)(2,1)}, u32[]{:S(2)}) copy-start(bf16[1,3,64,1280]{3,2,1,0:T(8,128)(2,1)} %param.8) | copy-start | bytes 1474564
  10.9 91.6 %all-to-all-start.2 = ((bf16[64,20,640]{2,1,0:T(8,128)(2,1)}), bf16[64,20,640]{2,1,0:T(8,128)(2,1)}, u32[]{:S(2)}, u32[]{:S(2)}) async-start(bf16[64,20,640]{2,1,0:T(8,128)(2,1)} %stack.2), calls=%async_computation.2 | async-start | bytes 3932160 | tf_op jit(solution)/shard_map/all_to_all | solution.py:106
  21.8 245.1 %all-gather.11.cloned.1.call-start = ((), (), s32[]{:S(2)}) async-start(), calls=%async_computation.11 | async-start | bytes 2662400 | tf_op jit(solution)/shard_map/all_gather | solution.py:109
  23.5 77.5 %copy-start.7 = (f32[1280]{0:T(1024)S(1)}, f32[1280]{0:T(1024)}, u32[]{:S(2)}) copy-start(f32[1280]{0:T(1024)} %param.11) | copy-start | bytes 15364
  100.9 1.5 copy-start.3
  102.5 20.0 %all-to-all-start.1 = ((bf16[3,64,640]{2,0,1:T(4,128)(2,1)}), bf16[3,64,640]{2,0,1:T(4,128)(2,1)S(1)}, u32[]{:S(2)}, u32[]{:S(2)}) async-start(bf16[3,64,640]{2,0,1:T(4,128)(2,1)} %copy.44), calls=%async_computation.1 | async-start | bytes 655360 | tf_op jit(solution)/shard_map/all_to_all | solution.py:124
  122.5 66.5 %all-to-all-start.3 = ((bf16[3,64,640]{2,0,1:T(4,128)(2,1)}), bf16[3,64,640]{2,0,1:T(4,128)(2,1)}, u32[]{:S(2)}, u32[]{:S(2)}) async-start(bf16[3,64,640]{2,0,1:T(4,128)(2,1)} %copy.45), calls=%async_computation.3 | async-start | bytes 655360 | tf_op jit(solution)/shard_map/all_to_all | solution.py:125
  189.0 85.2 %all-to-all-start = ((bf16[3,64,640]{2,0,1:T(4,128)(2,1)}), bf16[3,64,640]{2,0,1:T(4,128)(2,1)}, u32[]{:S(2)}, u32[]{:S(2)}) async-start(bf16[3,64,640]{2,0,1:T(4,128)(2,1)} %copy.43), calls=%async_computation | async-start | bytes 655360 | tf_op jit(solution)/shard_map/all_to_all | solution.py:126
  274.2 20.0 %all-to-all-start.5 = ((bf16[3,64,640]{2,0,1:T(4,128)(2,1)}), bf16[3,64,640]{2,0,1:T(4,128)(2,1)}, u32[]{:S(2)}, u32[]{:S(2)}) async-start(bf16[3,64,640]{2,0,1:T(4,128)(2,1)} %copy.52), calls=%async_computation.5 | async-start | bytes 655360 | tf_op jit(solution)/shard_map/all_to_all | solution.py:146
  315.1 20.9 %all-to-all-start.7 = ((bf16[64,2,960]{2,1,0:T(2,128)(2,1)}), bf16[64,2,960]{2,1,0:T(2,128)(2,1)}, u32[]{:S(2)}, u32[]{:S(2)}) async-start(bf16[64,2,960]{2,1,0:T(2,128)(2,1)} %reshape.349), calls=%async_computation.7 | async-start | bytes 524288 | tf_op jit(solution)/shard_map/all_to_all | solution.py:152
  336.0 21.1 %all-to-all-start.6 = ((bf16[64,2,960]{2,1,0:T(2,128)(2,1)}), bf16[64,2,960]{2,1,0:T(2,128)(2,1)}, u32[]{:S(2)}, u32[]{:S(2)}) async-start(bf16[64,2,960]{2,1,0:T(2,128)(2,1)} %reshape.347), calls=%async_computation.6 | async-start | bytes 524288 | tf_op jit(solution)/shard_map/all_to_all | solution.py:151
  357.1 34.6 %all-to-all-start.8 = ((bf16[64,2,960]{2,1,0:T(2,128)(2,1)}), bf16[64,2,960]{2,1,0:T(2,128)(2,1)}, u32[]{:S(2)}, u32[]{:S(2)}) async-start(bf16[64,2,960]{2,1,0:T(2,128)(2,1)} %reshape.351), calls=%async_computation.8 | async-start | bytes 524288 | tf_op jit(solution)/shard_map/all_to_all | solution.py:153
  391.6 22.1 %all-to-all-start.4 = ((bf16[64,2,960]{2,1,0:T(2,128)(2,1)}), bf16[64,2,960]{2,1,0:T(2,128)(2,1)}, u32[]{:S(2)}, u32[]{:S(2)}) async-start(bf16[64,2,960]{2,1,0:T(2,128)(2,1)} %reshape.345), calls=%async_computation.4 | async-start | bytes 524288 | tf_op jit(solution)/shard_map/all_to_all | solution.py:129
  409.2 2.1 copy-start.2
  413.1 4.6 copy-start.5
  420.0 317.1 %copy-start.4 = (bf16[640,1280]{1,0:T(8,128)(2,1)S(1)}, bf16[640,1280]{1,0:T(8,128)(2,1)}, u32[]{:S(2)}) copy-start(bf16[640,1280]{1,0:T(8,128)(2,1)} %reshape.339) | copy-start | bytes 4915204
  736.4 2.0 copy-start.6
Sparse Core Ops, SparseCore 0:
  11.2 87.1 all-gather.8
  101.7 80.6 all-gather.6
  185.8 81.1 all-gather.10
